TPU v7x, 32 devices: a whole 2x2x4 slice. The times are simulated.
32 devices in a mesh: dp: 8 (over z, x), head: 4 (over y, core).
Axes of the slice: x: 2, y: 2, z: 4, core: 2. Of those that a mesh axis runs over, the one named last changes fastest.
Arguments:
- inputs: bfloat16 [8, 1024, 1152], P('dp', 'head'), may hold values from -6 to 6
- segments: int32 [8, 1024], P('dp'), may hold values from 0 to 7, never falling along the last dimension, each value on 1 to 512 neighbouring positions
- cotangent: bfloat16 [8, 1024, 1152], P('dp', 'head'), may hold values from -6 to 6
- query_weight: bfloat16 [1152, 1024], replicated, may hold values from -0.1875 to 0.1875
- key_weight: bfloat16 [1152, 256], replicated, may hold values from -0.1875 to 0.1875
- value_weight: bfloat16 [1152, 256], replicated, may hold values from -0.1875 to 0.1875
- out_weight: bfloat16 [1024, 1152], replicated, may hold values from -0.1875 to 0.1875
- gate_weight: bfloat16 [1152, 6912], P(None, 'head'), may hold values from -0.1875 to 0.1875
- up_weight: bfloat16 [1152, 6912], P(None, 'head'), may hold values from -0.1875 to 0.1875
- down_weight: bfloat16 [6912, 1152], P('head'), may hold values from -0.078125 to 0.078125
- input_gain: float32 [1152], replicated, may hold values from 0.1 to 1.9
- query_gain: float32 [256], replicated, may hold values from 0.1 to 1.9
- key_gain: float32 [256], replicated, may hold values from 0.1 to 1.9
- attn_gain: float32 [1152], replicated, may hold values from 0.1 to 1.9
- pre_ff_gain: float32 [1152], replicated, may hold values from 0.1 to 1.9
- post_ff_gain: float32 [1152], replicated, may hold values from 0.1 to 1.9
Outputs:
- layer_output: bfloat16 [8, 1024, 1152], P('dp', 'head')
- input_grad: float32 [8, 1024, 1152], P('dp', 'head')
- query_weight_grad: float32 [1152, 1024], replicated
- key_weight_grad: float32 [1152, 256], replicated
- value_weight_grad: float32 [1152, 256], replicated
- out_weight_grad: float32 [1024, 1152], replicated
- gate_weight_grad: float32 [1152, 6912], P('dp', 'head')
- up_weight_grad: float32 [1152, 6912], P('dp', 'head')
- down_weight_grad: float32 [6912, 1152], P('head', 'dp')
- input_gain_grad: float32 [1152], replicated
- query_gain_grad: float32 [256], replicated
- key_gain_grad: float32 [256], replicated
- attn_gain_grad: float32 [1152], replicated
- pre_ff_gain_grad: float32 [1152], replicated
- post_ff_gain_grad: float32 [1152], replicated
Inputs may be any that keep to these rules, and one draw needn't show every extreme that they name: `segments`: within a row the document numbers never fall; each of the 8 documents has 1 to 512 tokens, and one has exactly 512.
All inputs are finite; a program needn't handle non-finite values.
Results may differ from a plain program's by a relative error of at most 0.02.
Values may be sent and summed in bfloat16 or wider, within the bound.
No kernel may reach another device: no remote copies, remote signals or barrier semaphores. Data moves between devices by JAX's collectives and lax.ppermute only.
A program may use at most 192 MiB of HBM per device.

v0:
```python
from functools import partial
import jax
import jax.numpy as jnp
from jax import lax
from jax.sharding import PartitionSpec as P

EPSILON = 1e-06
ROPE_BASE = 1000000.0
MASKED = -1e30


def for_sending(x):
    return jax.tree.map(lambda a: a.astype(jnp.bfloat16) if a.dtype == jnp.float32 else a, x)


def rms_norm(values, gain):
    return values * lax.rsqrt(jnp.mean(values * values, axis=-1, keepdims=True) + EPSILON) * gain


def positions_of(segment_ids):
    count = segment_ids.shape[0]
    position_index = jnp.arange(count, dtype=jnp.int32)
    previous = jnp.concatenate([segment_ids[:1] - 1, segment_ids[:-1]])
    starts = jnp.where(segment_ids != previous, position_index, 0)
    return position_index - lax.cummax(starts, axis=0)


def rotary(values, positions, sign):
    half_width = values.shape[-1] // 2
    frequency = ROPE_BASE ** (-2.0 * jnp.arange(half_width, dtype=jnp.float32) / values.shape[-1])
    angle = positions.astype(jnp.float32)[:, None] * frequency[None, :]
    cosine_part = jnp.cos(angle)
    sine_part = jnp.sin(angle) * sign
    if values.ndim == 3:
        cosine_part = cosine_part[:, None, :]
        sine_part = sine_part[:, None, :]
    leading = values[..., :half_width]
    trailing = values[..., half_width:]
    return jnp.concatenate(
        [
            leading * cosine_part - trailing * sine_part,
            trailing * cosine_part + leading * sine_part,
        ],
        axis=-1,
    )


def product(left, right):
    return jnp.dot(left, right, preferred_element_type=jnp.float32)


def product_tn(left, right):
    return lax.dot_general(
        left, right, (((0,), (0,)), ((), ())), preferred_element_type=jnp.float32
    )


def product_nt(left, right):
    return lax.dot_general(
        left, right, (((1,), (1,)), ((), ())), preferred_element_type=jnp.float32
    )


def shards(
    inputs,
    segments,
    cotangent,
    query_weight,
    key_weight,
    value_weight,
    out_weight,
    gate_weight,
    up_weight,
    down_weight,
    input_gain,
    query_gain,
    key_gain,
    attn_gain,
    pre_ff_gain,
    post_ff_gain,
):
    low_type = jnp.bfloat16
    tok_rows = inputs.shape[1]
    head_dim = key_weight.shape[1]
    query_heads = query_weight.shape[1] // head_dim
    seq_len = segments.shape[1]
    block_rows = min(512, seq_len)
    score_scale = head_dim ** (-0.5)
    gelu_tanh = partial(jax.nn.gelu, approximate=True)
    x_rows = inputs[0].astype(jnp.float32)
    segment_ids = segments[0]
    all_positions = positions_of(segment_ids)
    own_start = lax.axis_index("head") * tok_rows
    positions = lax.dynamic_slice_in_dim(all_positions, own_start, tok_rows)
    position_index = jnp.arange(seq_len, dtype=jnp.int32)
    normed, input_pull = jax.vjp(rms_norm, x_rows, input_gain)
    normed_low = normed.astype(low_type)
    q_proj = product(normed_low, query_weight).reshape(tok_rows, query_heads, head_dim)
    k_proj = product(normed_low, key_weight)
    v_low = product(normed_low, value_weight).astype(low_type)
    q_normed, query_pull = jax.vjp(rms_norm, q_proj, query_gain)
    k_normed, key_pull = jax.vjp(rms_norm, k_proj, key_gain)
    q_low = rotary(q_normed, positions, 1.0).astype(low_type)
    k_low = rotary(k_normed, positions, 1.0).astype(low_type)
    query_rows = lax.all_to_all(q_low, "head", split_axis=1, concat_axis=0, tiled=True)[:, 0, :]
    row_segments_all = jnp.take(segment_ids, position_index)
    key_rows, value_rows = (
        lax.all_gather(k_low, "head", axis=0, tiled=True),
        lax.all_gather(v_low, "head", axis=0, tiled=True),
    )

    def masked_scores(start_row):
        row_slice = query_rows[start_row : start_row + block_rows]
        raw_scores = product_nt(row_slice, key_rows) * score_scale
        row_ids = position_index[start_row : start_row + block_rows]
        row_segments = row_segments_all[start_row : start_row + block_rows]
        allowed = (row_segments[:, None] == segment_ids[None, :]) & (
            position_index[None, :] <= row_ids[:, None]
        )
        return jnp.where(allowed, raw_scores, MASKED)

    attended_blocks = []
    log_blocks = []
    for start_row in range(0, seq_len, block_rows):
        masked = masked_scores(start_row)
        row_max = jnp.max(masked, axis=1, keepdims=True)
        exponent = jnp.exp(masked - row_max)
        row_total = jnp.sum(exponent, axis=1, keepdims=True)
        probabilities = (exponent / row_total).astype(low_type)
        attended_blocks.append(product(probabilities, value_rows))
        log_blocks.append(row_max + jnp.log(row_total))
    attended_low = jnp.concatenate(attended_blocks, axis=0).astype(low_type)
    log_totals = jnp.concatenate(log_blocks, axis=0)
    mixed_rows = lax.all_to_all(
        attended_low[:, None, :], "head", split_axis=0, concat_axis=1, tiled=True
    )
    mixed_rows = mixed_rows.reshape(tok_rows, query_heads * head_dim)
    projected = product(mixed_rows, out_weight)
    attn_branch, attn_pull = jax.vjp(rms_norm, projected, attn_gain)
    after_attn = x_rows + attn_branch
    pre_normed, pre_pull = jax.vjp(rms_norm, after_attn, pre_ff_gain)
    rows_all = lax.all_gather(pre_normed.astype(low_type), "head", axis=0, tiled=True)
    gate_act = product(rows_all, gate_weight)
    up_act = product(rows_all, up_weight)
    gelu_gate, gelu_pull = jax.vjp(gelu_tanh, gate_act)
    hidden_low = (gelu_gate * up_act).astype(low_type)
    ff_out = lax.psum_scatter(
        product(
            lax.slice_in_dim(hidden_low, 0, tok_rows * lax.axis_size("head"), axis=0), down_weight
        ).astype(jnp.bfloat16),
        "head",
        scatter_dimension=0,
        tiled=True,
    ).astype(jnp.float32)
    post_branch, post_pull = jax.vjp(rms_norm, ff_out, post_ff_gain)
    layer_out = after_attn + post_branch
    out_grad = cotangent[0].astype(jnp.float32)
    ff_grad, post_gain_grad = post_pull(out_grad)
    ff_grad_all = lax.all_gather(for_sending(ff_grad.astype(low_type)), "head", axis=0, tiled=True)
    down_grad = product_tn(hidden_low, ff_grad_all)
    hidden_grad = product_nt(ff_grad_all, down_weight)
    up_grad_low = (hidden_grad * gelu_gate).astype(low_type)
    gate_grad_low = gelu_pull(hidden_grad * up_act)[0].astype(low_type)
    gate_grad = product_tn(rows_all, gate_grad_low)
    up_grad = product_tn(rows_all, up_grad_low)
    up_slice = lax.slice_in_dim(up_grad_low, 0, tok_rows * lax.axis_size("head"), axis=0)
    pre_grad = lax.psum_scatter(
        (product_nt(gate_grad_low, gate_weight) + product_nt(up_slice, up_weight)).astype(
            jnp.bfloat16
        ),
        "head",
        scatter_dimension=0,
        tiled=True,
    ).astype(jnp.float32)
    after_from_ff, pre_gain_grad = pre_pull(pre_grad)
    after_grad = out_grad + after_from_ff
    projected_grad, attn_gain_grad = attn_pull(after_grad)
    projected_low = projected_grad.astype(low_type)
    out_weight_grad = product_tn(mixed_rows, projected_low)
    mixed_grad = product_nt(projected_low, out_weight).astype(low_type)
    mixed_grad = mixed_grad.reshape(tok_rows, query_heads, head_dim)
    attended_grad = lax.all_to_all(mixed_grad, "head", split_axis=1, concat_axis=0, tiled=True)[
        :, 0, :
    ]
    query_blocks = []
    key_grad = jnp.zeros((seq_len, head_dim), jnp.float32)
    value_grad = jnp.zeros((seq_len, head_dim), jnp.float32)
    for start_row in range(0, seq_len, block_rows):
        masked = masked_scores(start_row)
        probabilities = jnp.exp(masked - log_totals[start_row : start_row + block_rows])
        grad_rows = attended_grad[start_row : start_row + block_rows]
        value_grad = value_grad + product_tn(probabilities.astype(low_type), grad_rows)
        prob_grad = product_nt(grad_rows, value_rows)
        row_delta = jnp.sum(prob_grad * probabilities, axis=1, keepdims=True)
        score_grad = (probabilities * (prob_grad - row_delta)).astype(low_type)
        query_blocks.append(product(score_grad, key_rows) * score_scale)
        key_grad = (
            key_grad
            + product_tn(score_grad, query_rows[start_row : start_row + block_rows]) * score_scale
        )
    query_grad_low = jnp.concatenate(query_blocks, axis=0).astype(low_type)
    query_back = lax.all_to_all(
        query_grad_low[:, None, :], "head", split_axis=0, concat_axis=1, tiled=True
    )
    key_share, value_share = (
        lax.psum_scatter(
            key_grad.astype(jnp.bfloat16), "head", scatter_dimension=0, tiled=True
        ).astype(jnp.float32),
        lax.psum_scatter(
            value_grad.astype(jnp.bfloat16), "head", scatter_dimension=0, tiled=True
        ).astype(jnp.float32),
    )
    q_proj_grad, query_gain_grad = query_pull(
        rotary(query_back.astype(jnp.float32), positions, -1.0)
    )
    key_back = key_share.astype(low_type).astype(jnp.float32)
    k_proj_grad, key_gain_grad = key_pull(rotary(key_back, positions, -1.0))
    q_grad_low = q_proj_grad.reshape(tok_rows, query_heads * head_dim).astype(low_type)
    k_grad_low = k_proj_grad.astype(low_type)
    v_grad_low = value_share.astype(low_type)
    query_weight_grad = product_tn(normed_low, q_grad_low)
    key_weight_grad = product_tn(normed_low, k_grad_low)
    value_weight_grad = product_tn(normed_low, v_grad_low)
    normed_grad = (
        product_nt(q_grad_low, query_weight)
        + product_nt(k_grad_low, key_weight)
        + product_nt(v_grad_low, value_weight)
    )
    input_from_norm, input_gain_grad = input_pull(normed_grad)
    input_grad = after_grad + input_from_norm
    summed = lax.psum(
        (
            query_weight_grad,
            key_weight_grad,
            value_weight_grad,
            out_weight_grad,
            input_gain_grad,
            query_gain_grad,
            key_gain_grad,
            attn_gain_grad,
            pre_gain_grad,
            post_gain_grad,
        ),
        ("dp", "head"),
    )
    gate_share, up_share, down_share = (
        lax.psum_scatter(
            gate_grad.astype(jnp.bfloat16), "dp", scatter_dimension=0, tiled=True
        ).astype(jnp.float32),
        lax.psum_scatter(
            up_grad.astype(jnp.bfloat16), "dp", scatter_dimension=0, tiled=True
        ).astype(jnp.float32),
        lax.psum_scatter(
            down_grad.astype(jnp.bfloat16), "dp", scatter_dimension=1, tiled=True
        ).astype(jnp.float32),
    )
    return (
        layer_out.astype(low_type)[None],
        input_grad[None],
        summed[0],
        summed[1],
        summed[2],
        summed[3],
        gate_share,
        up_share,
        down_share,
        summed[4],
        summed[5],
        summed[6],
        summed[7],
        summed[8],
        summed[9],
    )


def solution(mesh):
    in_specs = (
        P("dp", "head", None),
        P("dp", None),
        P("dp", "head", None),
        P(),
        P(),
        P(),
        P(),
        P(None, "head"),
        P(None, "head"),
        P("head", None),
        P(),
        P(),
        P(),
        P(),
        P(),
        P(),
    )
    out_specs = (
        P("dp", "head", None),
        P("dp", "head", None),
        P(),
        P(),
        P(),
        P(),
        P("dp", "head"),
        P("dp", "head"),
        P("head", "dp"),
        P(),
        P(),
        P(),
        P(),
        P(),
        P(),
    )
    return jax.shard_map(shards, mesh=mesh, in_specs=in_specs, out_specs=out_specs, check_vma=False)
```

profile of v0, /device:TPU:0, one launch (start us, length us, event | category | flops | bytes accessed | tf_op | source)
XLA Modules:
  0.0 871.8 jit_solution(2436494161311775190)
XLA Ops:
  13.7 4.4 copy.65
  18.1 3.6 multiply_reduce_fusion.8
  25.6 4.3 all-to-all-start
  30.5 9.1 %gather_fusion = s32[1024]{0:T(1024)} fusion(s32[1024]{0:T(1024)S(1)} %bitcast.161, s32[1024]{0:T(1024)} %iota_clamp_fusion), kind=kCustom, calls=%fused_computation | custom fusion | bytes 12288 | tf_op jit(solution)/shard_map/jit(_take)/gather | solution.py:106
  43.4 9.0 %all_gather.12 = bf16[1024,256]{0,1:T(8,128)(2,1)} all-gather(bf16[256,256]{0,1:T(8,128)(2,1)S(1)} %pad_maximum_fusion.5), channel_id=1, replica_groups=mesh['dp'=8,'head'=4] {'head'}, dimensions={0}, use_global_device_ids=true | all-gather | bytes 655360 | tf_op jit(solution)/shard_map/all_gather | solution.py:108
  52.5 7.3 all_gather.13
  75.3 12.3 %all_to_all.54 = bf16[4,2,32768]{2,1,0:T(2,128)(2,1)S(1)} all-to-all(bf16[4,2,32768]{2,1,0:T(2,128)(2,1)} %reshape.403), channel_id=1, replica_groups=mesh['dp'=8,'head'=4] {'head'}, dimensions={0} | all-to-all | bytes 1048576 | tf_op jit(solution)/shard_map/all_to_all | solution.py:134
  97.3 24.7 %all-gather.3.cloned.1.call-done = bf16[1024,1152]{1,0:T(8,128)(2,1)} async-done(((bf16[256,1152]{1,0:T(8,128)(2,1)}), bf16[1024,1152]{1,0:T(8,128)(2,1)}) %all-gather.3.cloned.1.call-update) | async-done | bytes 2359312 | tf_op jit(solution)/shard_map/all_gather | solution.py:142
  122.0 7.4 fusion.98
  129.5 7.9 multiply_convert_fusion.1
  139.1 6.3 convolution_convert_fusion.3
  145.5 32.9 %reduce-scatter.8.cloned.1.call-done = bf16[256,1152]{1,0:T(8,128)(2,1)} async-done(((bf16[1024,1152]{1,0:T(8,128)(2,1)}), bf16[256,1152]{1,0:T(8,128)(2,1)}) %reduce-scatter.8.cloned.1.call-update) | async-done | bytes 589840 | tf_op jit(solution)/shard_map/reduce_scatter | solution.py:147
  184.7 23.9 %all-gather.5.cloned.1.call-done = bf16[1024,1152]{1,0:T(8,128)(2,1)} async-done(((bf16[256,1152]{1,0:T(8,128)(2,1)}), bf16[1024,1152]{1,0:T(8,128)(2,1)}) %all-gather.5.cloned.1.call-update) | async-done | bytes 2359312 | tf_op jit(solution)/shard_map/all_gather | solution.py:159
  208.6 14.8 %multiply_convert_fusion = (bf16[1024,1728]{0,1:T(8,128)(2,1)S(1)}, bf16[1024,1728]{0,1:T(8,128)(2,1)S(1)}) fusion(f32[1024,1728]{0,1:T(8,128)} %copy-done.94, f32[1024,1728]{0,1:T(8,128)} %get-tuple-element.71, bf16[1024,1152]{1,0:T(8,128)(2,1)} %all-gather.5.cloned.1.call-done, bf16[1728,1152]{1,0:T(8,128)(2,1)} %param.25), kind=kOutput, calls=%fused_computation.13 | convolution fusion | flops 4119330816 | bytes 27574272 | tf_op jit(solution)/shard_map/dot_general | solution.py:59
  223.5 5.2 fusion.99
  228.7 6.8 add_convert_fusion
  235.6 33.0 %reduce-scatter.10.cloned.1.call-done = bf16[256,1152]{1,0:T(8,128)(2,1)} async-done(((bf16[1024,1152]{1,0:T(8,128)(2,1)}), bf16[256,1152]{1,0:T(8,128)(2,1)}) %reduce-scatter.10.cloned.1.call-update) | async-done | bytes 589840 | tf_op jit(solution)/shard_map/reduce_scatter | solution.py:167
  271.8 3.9 multiply_reduce_fusion.2
  277.8 4.3 all-to-all-start.2
  282.2 8.8 %all-to-all-done.2 = bf16[256,4,256]{2,0,1:T(8,128)(2,1)} async-done(((bf16[256,4,256]{2,0,1:T(8,128)(2,1)}), bf16[256,4,256]{2,0,1:T(8,128)(2,1)}, u32[]{:S(2)}, u32[]{:S(2)}) %all-to-all-start.2) | async-done | bytes 524320 | tf_op jit(solution)/shard_map/all_to_all | solution.py:182
  302.8 9.4 %convolution_convert_fusion = bf16[1728,1152]{0,1:T(8,128)(2,1)} fusion(bf16[1024,1728]{0,1:T(8,128)(2,1)} %copy-done.93, bf16[1024,1152]{1,0:T(8,128)(2,1)} %all-gather.5.cloned.1.call-done), kind=kOutput, calls=%fused_computation.3 | convolution fusion | flops 4078854144 | bytes 9879552 | tf_op jit(solution)/shard_map/dot_general | solution.py:53
  313.9 8.4 convolution_convert_fusion.1
  322.4 8.2 convolution_convert_fusion.2
  334.9 3.5 all-to-all-start.3
  341.5 8.0 all-to-all-done.3
  359.5 3.1 fusion.59
  367.3 42.1 %all-reduce = (f32[1152]{0:T(1024)}, f32[256]{0:T(256)}, f32[256]{0:T(256)}, f32[1152]{0:T(1024)}, f32[1152]{0:T(1024)}, /*index=5*/f32[1152]{0:T(1024)}) all-reduce(f32[1152]{0:T(1024)S(1)} %get-tuple-element.21, f32[256]{0:T(256)S(1)} %get-tuple-element.17, ...), channel_id=1, replica_groups=mesh['dp'=8,'head'=4] {'dp','head'}, use_global_device_ids=true, to_apply=%region_32.33 | all-reduce | flops 5120 | bytes 40960 | tf_op jit(solution)/shard_map/psum | solution.py:231
  410.7 29.7 %reduce-scatter.20.cloned.1.call-done = bf16[1728,144]{0,1:T(8,128)(2,1)} async-done(((bf16[1728,1152]{0,1:T(8,128)(2,1)}), bf16[1728,144]{0,1:T(8,128)(2,1)}) %reduce-scatter.20.cloned.1.call-update) | async-done | bytes 497680 | tf_op jit(solution)/shard_map/reduce_scatter | solution.py:253
  442.5 89.1 %reduce-scatter.18.cloned.1.call-done = bf16[144,1728]{1,0:T(8,128)(2,1)} async-done(((bf16[1152,1728]{1,0:T(8,128)(2,1)}), bf16[144,1728]{1,0:T(8,128)(2,1)}) %reduce-scatter.18.cloned.1.call-update) | async-done | bytes 497680 | tf_op jit(solution)/shard_map/reduce_scatter | solution.py:250
  533.7 89.1 %reduce-scatter.16.cloned.1.call-done = bf16[144,1728]{1,0:T(8,128)(2,1)} async-done(((bf16[1152,1728]{1,0:T(8,128)(2,1)}), bf16[144,1728]{1,0:T(8,128)(2,1)}) %reduce-scatter.16.cloned.1.call-update) | async-done | bytes 497680 | tf_op jit(solution)/shard_map/reduce_scatter | solution.py:247
  624.8 228.5 %all-reduce.4.cloned.1.call-done = (f32[1152,1024]{1,0:T(8,128)}, f32[1152,256]{1,0:T(8,128)}, f32[1152,256]{1,0:T(8,128)}, f32[1024,1152]{1,0:T(8,128)}) async-done(((f32[1152,1024]{1,0:T(8,128)}, f32[1152,256]{1,0:T(8,128)}, f32[1152,256]{1,0:T(8,128)}, f32[1024,1152]{1,0:T(8,128)}), (f32[1152,1024]{1,0:T(8,128)}, f32[1152,256]{1,0:T(8,128)}, f32[1152,256]{1,0:T(8,128)}, ...) | async-done | bytes 11796496 | tf_op jit(solution)/shard_map/psum | solution.py:231
  853.3 5.4 copy.76
  (322 shorter events, 101.5 us)
Async XLA Ops:
  7.2 85.5 %copy-start = (bf16[1024,1152]{1,0:T(8,128)(2,1)S(1)}, bf16[1024,1152]{1,0:T(8,128)(2,1)}, u32[]{:S(2)}) copy-start(bf16[1024,1152]{1,0:T(8,128)(2,1)} %param.22) | copy-start | bytes 7077892
  7.2 14.8 %copy-start.84 = (f32[128]{0:T(128)}, f32[128]{0:T(128)S(1)}, u32[]{:S(2)}) copy-start(f32[128]{0:T(128)S(1)} %multiply_power_fusion) | copy-start | bytes 1540
  9.8 8.3 copy-start.50
  13.7 8.2 copy-start.27
  13.7 8.1 copy-start.55
  25.6 34.1 %all-to-all-start = ((bf16[256,4,256]{0,2,1:T(8,128)(2,1)}), bf16[256,4,256]{0,2,1:T(8,128)(2,1)}, u32[]{:S(2)}, u32[]{:S(2)}) async-start(bf16[256,4,256]{0,2,1:T(8,128)(2,1)} %pad_maximum_fusion.1), calls=%async_computation | async-start | bytes 1048576 | tf_op jit(solution)/shard_map/all_to_all | solution.py:105
  29.9 92.1 %all-gather.3.cloned.1.call-start = ((), (), s32[]{:S(2)}) async-start(), calls=%async_computation.11 | async-start | bytes 2949120 | tf_op jit(solution)/shard_map/all_gather | solution.py:142
  30.5 10.9 %copy-start.40 = (bf16[1152,256]{1,0:T(8,128)(2,1)S(1)}, bf16[1152,256]{1,0:T(8,128)(2,1)}, u32[]{:S(2)}) copy-start(bf16[1152,256]{1,0:T(8,128)(2,1)} %param.21) | copy-start | bytes 1769476
  42.5 22.8 %copy-start.83 = (s32[512]{0:T(512)S(1)}, s32[512]{0:T(512)}, u32[]{:S(2)}) copy-start(s32[512]{0:T(512)} %slice.99) | copy-start | bytes 6148
  59.7 10.6 %copy-start.19 = (bf16[1024,256]{1,0:T(8,128)(2,1)}, bf16[1024,256]{1,0:T(8,128)(2,1)S(1)}, u32[]{:S(2)}) copy-start(bf16[1024,256]{1,0:T(8,128)(2,1)S(1)} %all_gather.13) | copy-start | bytes 1572868
  95.1 34.3 %copy-start.63 = (f32[256]{0:T(256)}, f32[256]{0:T(256)S(1)}, u32[]{:S(2)}) copy-start(f32[256]{0:T(256)S(1)} %get-tuple-element.38) | copy-start | bytes 3076
  95.1 34.3 %copy-start.59 = (f32[256]{0:T(256)}, f32[256]{0:T(256)S(1)}, u32[]{:S(2)}) copy-start(f32[256]{0:T(256)S(1)} %fusion.83) | copy-start | bytes 3076
  97.1 81.3 %reduce-scatter.8.cloned.1.call-start = ((), (), s32[]{:S(2)}) async-start(), calls=%async_computation.12 | async-start | bytes 2949120 | tf_op jit(solution)/shard_map/reduce_scatter | solution.py:147
  129.5 7.9 copy-start.94
  129.5 9.6 %copy-start.86 = (bf16[1728,1152]{1,0:T(8,128)(2,1)S(1)}, bf16[1728,1152]{1,0:T(8,128)(2,1)}, u32[]{:S(2)}) copy-start(bf16[1728,1152]{1,0:T(8,128)(2,1)} %param.25) | copy-start | bytes 11943940
  145.5 63.1 %all-gather.5.cloned.1.call-start = ((), (), s32[]{:S(2)}) async-start(), calls=%async_computation.13 | async-start | bytes 2949120 | tf_op jit(solution)/shard_map/all_gather | solution.py:159
  184.4 84.1 %reduce-scatter.10.cloned.1.call-start = ((), (), s32[]{:S(2)}) async-start(), calls=%async_computation.14 | async-start | bytes 2949120 | tf_op jit(solution)/shard_map/reduce_scatter | solution.py:167
  208.6 14.9 %copy-start.87 = (bf16[1152,1728]{0,1:T(8,128)(2,1)S(1)}, bf16[1152,1728]{0,1:T(8,128)(2,1)}, u32[]{:S(2)}) copy-start(bf16[1152,1728]{0,1:T(8,128)(2,1)} %param.23) | copy-start | bytes 11943940
  276.9 15.1 %copy-start.7 = (f32[512,1024]{1,0:T(8,128)S(1)}, f32[512,1024]{1,0:T(8,128)}, u32[]{:S(2)}) copy-start(f32[512,1024]{1,0:T(8,128)} %copy-done.6) | copy-start | bytes 6291460
  276.9 15.1 %copy-start.20 = (bf16[1024,256]{1,0:T(8,128)(2,1)S(1)}, bf16[1024,256]{1,0:T(8,128)(2,1)}, u32[]{:S(2)}) copy-start(bf16[1024,256]{1,0:T(8,128)(2,1)} %copy-done.19) | copy-start | bytes 1572868
  277.8 13.2 %all-to-all-start.2 = ((bf16[256,4,256]{2,0,1:T(8,128)(2,1)}), bf16[256,4,256]{2,0,1:T(8,128)(2,1)}, u32[]{:S(2)}, u32[]{:S(2)}) async-start(bf16[256,4,256]{2,0,1:T(8,128)(2,1)} %bitcast.179), calls=%async_computation.4 | async-start | bytes 1048576 | tf_op jit(solution)/shard_map/all_to_all | solution.py:182
  282.1 69.2 %reduce-scatter.12.cloned.1.call-start = ((), (), s32[]{:S(2)}) async-start(), calls=%async_computation.15 | async-start | bytes 655360 | tf_op jit(solution)/shard_map/reduce_scatter | solution.py:206
  299.0 58.1 %reduce-scatter.14.cloned.1.call-start = ((), (), s32[]{:S(2)}) async-start(), calls=%async_computation.16 | async-start | bytes 655360 | tf_op jit(solution)/shard_map/reduce_scatter | solution.py:209
  302.8 137.7 %reduce-scatter.20.cloned.1.call-start = ((), (), s32[]{:S(2)}) async-start(), calls=%async_computation.19 | async-start | bytes 4644864 | tf_op jit(solution)/shard_map/reduce_scatter | solution.py:253
  312.2 219.4 %reduce-scatter.18.cloned.1.call-start = ((), (), s32[]{:S(2)}) async-start(), calls=%async_computation.18 | async-start | bytes 4644864 | tf_op jit(solution)/shard_map/reduce_scatter | solution.py:250
  322.3 300.4 %reduce-scatter.16.cloned.1.call-start = ((), (), s32[]{:S(2)}) async-start(), calls=%async_computation.17 | async-start | bytes 4644864 | tf_op jit(solution)/shard_map/reduce_scatter | solution.py:247
  334.9 14.6 %all-to-all-start.3 = ((bf16[4,2,32768]{2,1,0:T(2,128)(2,1)}), bf16[4,2,32768]{2,1,0:T(2,128)(2,1)S(1)}, u32[]{:S(2)}, u32[]{:S(2)}) async-start(bf16[4,2,32768]{2,1,0:T(2,128)(2,1)} %reshape.405), calls=%async_computation.5 | async-start | bytes 1048576 | tf_op jit(solution)/shard_map/all_to_all | solution.py:202
  338.4 514.9 %all-reduce.4.cloned.1.call-start = ((), (), s32[]{:S(2)}) async-start(), calls=%async_computation.20 | async-start | bytes 23592960 | tf_op jit(solution)/shard_map/psum | solution.py:231
  366.6 42.8 %copy-start.69 = (f32[256]{0:T(256)S(1)}, f32[256]{0:T(256)}, u32[]{:S(2)}) copy-start(f32[256]{0:T(256)} %copy-done.68) | copy-start | bytes 3076
  366.6 42.8 %copy-start.12 = (f32[256,1152]{1,0:T(8,128)S(1)}, f32[256,1152]{1,0:T(8,128)}, u32[]{:S(2)}) copy-start(f32[256,1152]{1,0:T(8,128)} %copy-done.11) | copy-start | bytes 3538948
  853.3 8.1 slice-start
  853.3 8.1 slice-start.1
  (79 other events, 213.4 us)
Sparse Core Ops, SparseCore 0:
  97.2 24.7 all-gather.2
  145.6 32.8 reduce-scatter.7
  184.5 24.0 all-gather.4
  235.7 32.8 reduce-scatter.9
  299.1 21.6 reduce-scatter.11
  323.2 24.2 reduce-scatter.13
  351.0 89.3 reduce-scatter.19
  444.0 87.5 reduce-scatter.17
  535.2 87.5 reduce-scatter.15
  629.6 223.6 all-reduce.3
where the time goes:
time: 881 us; the launch traced here: 872 us
  waiting for transfers between devices  568 us (64%)
  matrix products  106 us (12%)
  blocking collectives  70.7 us (8%)
  local copies, waits for them, and re-layouts  59.4 us (7%)
  other arithmetic  39 us (4%)
  between operations  16.2 us (2%)
  starting transfers between devices  12.8 us (1%)
    psum x1, waiting for transfers between devices, shards(): lax.psum((query_weight_grad, key_weight_grad, value_weight_grad, out_weig...  228 us
    reduce_scatter x1, waiting for transfers between devices, shards(): lax.psum_scatter(gate_grad.astype(jnp.bfloat16), 'dp', scatter_dimension=...  89.1 us
    reduce_scatter x1, waiting for transfers between devices, shards(): lax.psum_scatter(up_grad.astype(jnp.bfloat16), 'dp', scatter_dimension=0,...  89.1 us
    psum x1, blocking collectives, shards(): lax.psum((query_weight_grad, key_weight_grad, value_weight_grad, out_weig...  42.1 us
    dot_general x11, matrix products, product_tn(): lax.dot_general(left, right, (((0,), (0,)), ((), ())), preferred_element_...  41.5 us
    dot_general x11, matrix products, product_nt(): lax.dot_general(left, right, (((1,), (1,)), ((), ())), preferred_element_...  33.4 us
    reduce_scatter x1, waiting for transfers between devices, shards(): lax.psum_scatter((product_nt(gate_grad_low, gate_weight) + product_nt(up_...  33 us
    reduce_scatter x1, waiting for transfers between devices, shards(): lax.psum_scatter(product(lax.slice_in_dim(hidden_low, 0, tok_rows * lax.a...  32.9 us
  transfers between devices with their start and end apart: 13, of which 10 were waited for; matrix products, arithmetic and copies ran while one was open for 8% of the time, Pallas kernels for 0%

commit v1 on v0

--- a/solution.py
+++ b/solution.py
@@ -139,7 +139,16 @@
     attn_branch, attn_pull = jax.vjp(rms_norm, projected, attn_gain)
     after_attn = x_rows + attn_branch
     pre_normed, pre_pull = jax.vjp(rms_norm, after_attn, pre_ff_gain)
-    rows_all = lax.all_gather(pre_normed.astype(low_type), "head", axis=0, tiled=True)
+    inp = pre_normed.astype(low_type)
+    rows_all = jnp.concatenate(
+        lax.all_to_all(
+            jnp.stack([inp] * lax.psum(1, axis_name="head"), axis=0),
+            axis_name="head",
+            split_axis=0,
+            concat_axis=0,
+        ),
+        axis=0,
+    )
     gate_act = product(rows_all, gate_weight)
     up_act = product(rows_all, up_weight)
     gelu_gate, gelu_pull = jax.vjp(gelu_tanh, gate_act)

time: 881 us -> 885 us (level)
  blocking collectives: 70.7 us -> 102 us
  waiting for transfers between devices: 568 us -> 544 us
    all_to_all x0 -> x1, blocking collectives: none -> 31.4 us  [shards(): lax.all_to_all(jnp.stack([inp] * lax.psum(1, axis_name='head'), axis=0),...]
    all_gather x1 -> x0, waiting for transfers between devices: 24.7 us -> none  [shards(): lax.all_gather(pre_normed.astype(low_type), 'head', axis=0, tiled=True)]
    unnamed x205 -> x207, local copies, waits for them, and re-layouts: 32.8 us -> 32.8 us
  transfers between devices with their start and end apart: 13 -> 12, of which waited for: 10 -> 9; matrix products, arithmetic and copies ran while one was open for 8% -> 8% of each run, Pallas kernels for 0% -> 0%
where the time goes in v1:
time: 885 us; the launch traced here: 876 us
  waiting for transfers between devices  544 us (61%)
  matrix products  103 us (12%)
  blocking collectives  102 us (12%)
  local copies, waits for them, and re-layouts  59.6 us (7%)
  other arithmetic  38.2 us (4%)
  between operations  15.9 us (2%)
  starting transfers between devices  12.6 us (1%)
    psum x1, waiting for transfers between devices, shards(): lax.psum((query_weight_grad, key_weight_grad, value_weight_grad, out_weig...  229 us
    reduce_scatter x1, waiting for transfers between devices, shards(): lax.psum_scatter(gate_grad.astype(jnp.bfloat16), 'dp', scatter_dimension=...  89.1 us
    reduce_scatter x1, waiting for transfers between devices, shards(): lax.psum_scatter(up_grad.astype(jnp.bfloat16), 'dp', scatter_dimension=0,...  89.1 us
    psum x1, blocking collectives, shards(): lax.psum((query_weight_grad, key_weight_grad, value_weight_grad, out_weig...  42.2 us
    dot_general x11, matrix products, product_tn(): lax.dot_general(left, right, (((0,), (0,)), ((), ())), preferred_element_...  41.5 us
    reduce_scatter x1, waiting for transfers between devices, shards(): lax.psum_scatter(product(lax.slice_in_dim(hidden_low, 0, tok_rows * lax.a...  33.6 us
    dot_general x11, matrix products, product_nt(): lax.dot_general(left, right, (((1,), (1,)), ((), ())), preferred_element_...  33.4 us
    reduce_scatter x1, waiting for transfers between devices, shards(): lax.psum_scatter((product_nt(gate_grad_low, gate_weight) + product_nt(up_...  33 us
  transfers between devices with their start and end apart: 12, of which 9 were waited for; matrix products, arithmetic and copies ran while one was open for 8% of the time, Pallas kernels for 0%

profile of v1, /device:TPU:0, one launch (start us, length us, event | category | flops | bytes accessed | tf_op | source)
XLA Modules:
  0.0 876.0 jit_solution(11442087228360037804)
XLA Ops:
  13.7 4.4 copy.65
  18.1 3.6 multiply_reduce_fusion.8
  25.6 4.3 all-to-all-start
  30.5 9.1 %gather_fusion = s32[1024]{0:T(1024)} fusion(s32[1024]{0:T(1024)S(1)} %bitcast.162, s32[1024]{0:T(1024)} %iota_clamp_fusion), kind=kCustom, calls=%fused_computation | custom fusion | bytes 12288 | tf_op jit(solution)/shard_map/jit(_take)/gather | solution.py:106
  43.4 9.0 %all_gather.9 = bf16[1024,256]{0,1:T(8,128)(2,1)} all-gather(bf16[256,256]{0,1:T(8,128)(2,1)S(1)} %pad_maximum_fusion.5), channel_id=1, replica_groups=mesh['dp'=8,'head'=4] {'head'}, dimensions={0}, use_global_device_ids=true | all-gather | bytes 655360 | tf_op jit(solution)/shard_map/all_gather | solution.py:108
  52.5 7.3 all_gather.10
  75.2 12.3 %all_to_all.59 = bf16[4,2,32768]{2,1,0:T(2,128)(2,1)S(1)} all-to-all(bf16[4,2,32768]{2,1,0:T(2,128)(2,1)} %reshape.409), channel_id=1, replica_groups=mesh['dp'=8,'head'=4] {'head'}, dimensions={0} | all-to-all | bytes 1048576 | tf_op jit(solution)/shard_map/all_to_all | solution.py:134
  96.4 31.4 %all_to_all.60 = bf16[4,256,1152]{2,1,0:T(8,128)(2,1)S(1)} all-to-all(bf16[4,256,1152]{2,1,0:T(8,128)(2,1)S(1)} %stack.2), channel_id=1, replica_groups=mesh['dp'=8,'head'=4] {'head'}, dimensions={0} | all-to-all | bytes 4718592 | tf_op jit(solution)/shard_map/all_to_all | solution.py:144
  127.8 4.9 fusion.98
  132.8 7.9 multiply_convert_fusion.1
  142.4 6.3 convolution_convert_fusion.3
  148.8 33.6 %reduce-scatter.8.cloned.1.call-done = bf16[256,1152]{1,0:T(8,128)(2,1)} async-done(((bf16[1024,1152]{1,0:T(8,128)(2,1)}), bf16[256,1152]{1,0:T(8,128)(2,1)}) %reduce-scatter.8.cloned.1.call-update) | async-done | bytes 589840 | tf_op jit(solution)/shard_map/reduce_scatter | solution.py:156
  188.7 23.9 %all-gather.2.cloned.1.call-done = bf16[1024,1152]{1,0:T(8,128)(2,1)} async-done(((bf16[256,1152]{1,0:T(8,128)(2,1)}), bf16[1024,1152]{1,0:T(8,128)(2,1)}) %all-gather.2.cloned.1.call-update) | async-done | bytes 2359312 | tf_op jit(solution)/shard_map/all_gather | solution.py:168
  212.6 14.8 %multiply_convert_fusion = (bf16[1024,1728]{0,1:T(8,128)(2,1)S(1)}, bf16[1024,1728]{0,1:T(8,128)(2,1)S(1)}) fusion(f32[1024,1728]{0,1:T(8,128)} %copy-done.95, f32[1024,1728]{0,1:T(8,128)} %get-tuple-element.71, bf16[1024,1152]{1,0:T(8,128)(2,1)} %all-gather.2.cloned.1.call-done, bf16[1728,1152]{1,0:T(8,128)(2,1)} %param.25), kind=kOutput, calls=%fused_computation.13 | convolution fusion | flops 4119330816 | bytes 27574272 | tf_op jit(solution)/shard_map/dot_general | solution.py:59
  227.5 5.2 fusion.99
  232.7 6.8 add_convert_fusion
  239.6 33.0 %reduce-scatter.10.cloned.1.call-done = bf16[256,1152]{1,0:T(8,128)(2,1)} async-done(((bf16[1024,1152]{1,0:T(8,128)(2,1)}), bf16[256,1152]{1,0:T(8,128)(2,1)}) %reduce-scatter.10.cloned.1.call-update) | async-done | bytes 589840 | tf_op jit(solution)/shard_map/reduce_scatter | solution.py:176
  275.8 3.9 multiply_reduce_fusion.2
  281.8 4.3 all-to-all-start.3
  286.2 8.8 all-to-all-done.3
  306.8 9.4 %convolution_convert_fusion = bf16[1728,1152]{0,1:T(8,128)(2,1)} fusion(bf16[1024,1728]{0,1:T(8,128)(2,1)} %copy-done.94, bf16[1024,1152]{1,0:T(8,128)(2,1)} %all-gather.2.cloned.1.call-done), kind=kOutput, calls=%fused_computation.3 | convolution fusion | flops 4078854144 | bytes 9879552 | tf_op jit(solution)/shard_map/dot_general | solution.py:53
  317.9 8.4 convolution_convert_fusion.1
  326.4 8.2 convolution_convert_fusion.2
  338.9 3.5 all-to-all-start.4
  345.5 7.9 all-to-all-done.4
  363.6 3.1 fusion.59
  371.3 42.2 %all-reduce = (f32[1152]{0:T(1024)}, f32[256]{0:T(256)}, f32[256]{0:T(256)}, f32[1152]{0:T(1024)}, f32[1152]{0:T(1024)}, /*index=5*/f32[1152]{0:T(1024)}) all-reduce(f32[1152]{0:T(1024)S(1)} %get-tuple-element.21, f32[256]{0:T(256)S(1)} %get-tuple-element.17, ...), channel_id=1, replica_groups=mesh['dp'=8,'head'=4] {'dp','head'}, use_global_device_ids=true, to_apply=%region_32.33 | all-reduce | flops 5120 | bytes 40960 | tf_op jit(solution)/shard_map/psum | solution.py:240
  414.8 29.4 %reduce-scatter.20.cloned.1.call-done = bf16[1728,144]{0,1:T(8,128)(2,1)} async-done(((bf16[1728,1152]{0,1:T(8,128)(2,1)}), bf16[1728,144]{0,1:T(8,128)(2,1)}) %reduce-scatter.20.cloned.1.call-update) | async-done | bytes 497680 | tf_op jit(solution)/shard_map/reduce_scatter | solution.py:262
  446.2 89.1 %reduce-scatter.18.cloned.1.call-done = bf16[144,1728]{1,0:T(8,128)(2,1)} async-done(((bf16[1152,1728]{1,0:T(8,128)(2,1)}), bf16[144,1728]{1,0:T(8,128)(2,1)}) %reduce-scatter.18.cloned.1.call-update) | async-done | bytes 497680 | tf_op jit(solution)/shard_map/reduce_scatter | solution.py:259
  537.4 89.1 %reduce-scatter.16.cloned.1.call-done = bf16[144,1728]{1,0:T(8,128)(2,1)} async-done(((bf16[1152,1728]{1,0:T(8,128)(2,1)}), bf16[144,1728]{1,0:T(8,128)(2,1)}) %reduce-scatter.16.cloned.1.call-update) | async-done | bytes 497680 | tf_op jit(solution)/shard_map/reduce_scatter | solution.py:256
  628.5 229.3 %all-reduce.4.cloned.1.call-done = (f32[1152,1024]{1,0:T(8,128)}, f32[1152,256]{1,0:T(8,128)}, f32[1152,256]{1,0:T(8,128)}, f32[1024,1152]{1,0:T(8,128)}) async-done(((f32[1152,1024]{1,0:T(8,128)}, f32[1152,256]{1,0:T(8,128)}, f32[1152,256]{1,0:T(8,128)}, f32[1024,1152]{1,0:T(8,128)}), (f32[1152,1024]{1,0:T(8,128)}, f32[1152,256]{1,0:T(8,128)}, f32[1152,256]{1,0:T(8,128)}, ...) | async-done | bytes 11796496 | tf_op jit(solution)/shard_map/psum | solution.py:240
  857.8 5.4 copy.76
  (323 shorter events, 100.6 us)
Async XLA Ops:
  7.2 85.5 %copy-start = (bf16[1024,1152]{1,0:T(8,128)(2,1)S(1)}, bf16[1024,1152]{1,0:T(8,128)(2,1)}, u32[]{:S(2)}) copy-start(bf16[1024,1152]{1,0:T(8,128)(2,1)} %param.22) | copy-start | bytes 7077892
  7.2 14.8 %copy-start.86 = (f32[128]{0:T(128)}, f32[128]{0:T(128)S(1)}, u32[]{:S(2)}) copy-start(f32[128]{0:T(128)S(1)} %multiply_power_fusion) | copy-start | bytes 1540
  9.8 8.3 copy-start.52
  13.7 8.2 copy-start.27
  13.7 8.1 copy-start.57
  25.6 34.1 %all-to-all-start = ((bf16[256,4,256]{0,2,1:T(8,128)(2,1)}), bf16[256,4,256]{0,2,1:T(8,128)(2,1)}, u32[]{:S(2)}, u32[]{:S(2)}) async-start(bf16[256,4,256]{0,2,1:T(8,128)(2,1)} %pad_maximum_fusion.1), calls=%async_computation | async-start | bytes 1048576 | tf_op jit(solution)/shard_map/all_to_all | solution.py:105
  29.9 152.6 %reduce-scatter.8.cloned.1.call-start = ((), (), s32[]{:S(2)}) async-start(), calls=%async_computation.12 | async-start | bytes 2949120 | tf_op jit(solution)/shard_map/reduce_scatter | solution.py:156
  30.5 10.9 %copy-start.42 = (bf16[1152,256]{1,0:T(8,128)(2,1)S(1)}, bf16[1152,256]{1,0:T(8,128)(2,1)}, u32[]{:S(2)}) copy-start(bf16[1152,256]{1,0:T(8,128)(2,1)} %param.21) | copy-start | bytes 1769476
  42.5 22.8 %copy-start.85 = (s32[512]{0:T(512)S(1)}, s32[512]{0:T(512)}, u32[]{:S(2)}) copy-start(s32[512]{0:T(512)} %slice.99) | copy-start | bytes 6148
  59.7 10.6 %copy-start.19 = (bf16[1024,256]{1,0:T(8,128)(2,1)}, bf16[1024,256]{1,0:T(8,128)(2,1)S(1)}, u32[]{:S(2)}) copy-start(bf16[1024,256]{1,0:T(8,128)(2,1)S(1)} %all_gather.10) | copy-start | bytes 1572868
  96.4 31.4 %copy-start.89 = (bf16[1152,1728]{0,1:T(8,128)(2,1)S(1)}, bf16[1152,1728]{0,1:T(8,128)(2,1)}, u32[]{:S(2)}) copy-start(bf16[1152,1728]{0,1:T(8,128)(2,1)} %param.23) | copy-start | bytes 11943940
  132.8 7.9 copy-start.95
  132.8 9.6 %copy-start.88 = (bf16[1728,1152]{1,0:T(8,128)(2,1)S(1)}, bf16[1728,1152]{1,0:T(8,128)(2,1)}, u32[]{:S(2)}) copy-start(bf16[1728,1152]{1,0:T(8,128)(2,1)} %param.25) | copy-start | bytes 11943940
  148.8 63.9 %all-gather.2.cloned.1.call-start = ((), (), s32[]{:S(2)}) async-start(), calls=%async_computation.13 | async-start | bytes 2949120 | tf_op jit(solution)/shard_map/all_gather | solution.py:168
  188.4 84.1 %reduce-scatter.10.cloned.1.call-start = ((), (), s32[]{:S(2)}) async-start(), calls=%async_computation.14 | async-start | bytes 2949120 | tf_op jit(solution)/shard_map/reduce_scatter | solution.py:176
  212.6 14.9 %copy-start.90 = (bf16[1152,1728]{0,1:T(8,128)(2,1)S(1)}, bf16[1152,1728]{0,1:T(8,128)(2,1)}, u32[]{:S(2)}) copy-start(bf16[1152,1728]{0,1:T(8,128)(2,1)} %param.23) | copy-start | bytes 11943940
  280.0 6.1 copy-start.79
  280.0 6.1 copy-start.81
  280.9 15.1 %copy-start.7 = (f32[512,1024]{1,0:T(8,128)S(1)}, f32[512,1024]{1,0:T(8,128)}, u32[]{:S(2)}) copy-start(f32[512,1024]{1,0:T(8,128)} %copy-done.6) | copy-start | bytes 6291460
  280.9 15.1 %copy-start.20 = (bf16[1024,256]{1,0:T(8,128)(2,1)S(1)}, bf16[1024,256]{1,0:T(8,128)(2,1)}, u32[]{:S(2)}) copy-start(bf16[1024,256]{1,0:T(8,128)(2,1)} %copy-done.19) | copy-start | bytes 1572868
  281.8 13.2 %all-to-all-start.3 = ((bf16[256,4,256]{2,0,1:T(8,128)(2,1)}), bf16[256,4,256]{2,0,1:T(8,128)(2,1)}, u32[]{:S(2)}, u32[]{:S(2)}) async-start(bf16[256,4,256]{2,0,1:T(8,128)(2,1)} %bitcast.184), calls=%async_computation.5 | async-start | bytes 1048576 | tf_op jit(solution)/shard_map/all_to_all | solution.py:191
  286.1 69.2 %reduce-scatter.12.cloned.1.call-start = ((), (), s32[]{:S(2)}) async-start(), calls=%async_computation.15 | async-start | bytes 655360 | tf_op jit(solution)/shard_map/reduce_scatter | solution.py:215
  303.0 58.1 %reduce-scatter.14.cloned.1.call-start = ((), (), s32[]{:S(2)}) async-start(), calls=%async_computation.16 | async-start | bytes 655360 | tf_op jit(solution)/shard_map/reduce_scatter | solution.py:218
  306.8 137.4 %reduce-scatter.20.cloned.1.call-start = ((), (), s32[]{:S(2)}) async-start(), calls=%async_computation.19 | async-start | bytes 4644864 | tf_op jit(solution)/shard_map/reduce_scatter | solution.py:262
  316.2 219.1 %reduce-scatter.18.cloned.1.call-start = ((), (), s32[]{:S(2)}) async-start(), calls=%async_computation.18 | async-start | bytes 4644864 | tf_op jit(solution)/shard_map/reduce_scatter | solution.py:259
  326.3 300.1 %reduce-scatter.16.cloned.1.call-start = ((), (), s32[]{:S(2)}) async-start(), calls=%async_computation.17 | async-start | bytes 4644864 | tf_op jit(solution)/shard_map/reduce_scatter | solution.py:256
  338.9 14.5 %all-to-all-start.4 = ((bf16[4,2,32768]{2,1,0:T(2,128)(2,1)}), bf16[4,2,32768]{2,1,0:T(2,128)(2,1)S(1)}, u32[]{:S(2)}, u32[]{:S(2)}) async-start(bf16[4,2,32768]{2,1,0:T(2,128)(2,1)} %reshape.411), calls=%async_computation.6 | async-start | bytes 1048576 | tf_op jit(solution)/shard_map/all_to_all | solution.py:211
  342.4 515.4 %all-reduce.4.cloned.1.call-start = ((), (), s32[]{:S(2)}) async-start(), calls=%async_computation.20 | async-start | bytes 23592960 | tf_op jit(solution)/shard_map/psum | solution.py:240
  370.6 42.9 %copy-start.71 = (f32[256]{0:T(256)S(1)}, f32[256]{0:T(256)}, u32[]{:S(2)}) copy-start(f32[256]{0:T(256)} %copy-done.70) | copy-start | bytes 3076
  370.6 42.9 %copy-start.12 = (f32[256,1152]{1,0:T(8,128)S(1)}, f32[256,1152]{1,0:T(8,128)}, u32[]{:S(2)}) copy-start(f32[256,1152]{1,0:T(8,128)} %copy-done.11) | copy-start | bytes 3538948
  857.8 8.1 slice-start
  857.8 8.1 slice-start.1
  (79 other events, 198.7 us)
Sparse Core Ops, SparseCore 0:
  148.9 33.5 reduce-scatter.7
  188.6 24.0 all-gather.1
  239.7 32.8 reduce-scatter.9
  303.1 21.6 reduce-scatter.11
  327.1 24.2 reduce-scatter.13
  354.9 89.2 reduce-scatter.19
  447.7 87.5 reduce-scatter.17
  538.9 87.5 reduce-scatter.15
  633.4 224.3 all-reduce.3
